TPU v7x, 32 devices: a whole 2x2x4 slice. The times are simulated.
32 devices in a mesh: wide: 8 (over z, x), narrow: 4 (over y, core).
Axes of the slice: x: 2, y: 2, z: 4, core: 2. Of those that a mesh axis runs over, the one named last changes fastest.
Arguments:
- flow_field: bfloat16 [64, 64, 16, 512], P('wide', 'narrow'), may hold values from -48 to 48
- fluid_mask: int32 [64, 64, 16], P('wide', 'narrow'), may hold values 0 or 1
- conv_weight: float32 [27, 512], replicated, may hold values from -1 to 1
- latents: bfloat16 [1024, 512], replicated, may hold values from -6 to 6
- w_query1: bfloat16 [512, 512], replicated, may hold values from -0.25 to 0.25
- w_key1: bfloat16 [512, 512], replicated, may hold values from -0.25 to 0.25
- w_value1: bfloat16 [512, 512], replicated, may hold values from -0.25 to 0.25
- w_out1: bfloat16 [512, 512], replicated, may hold values from -0.25 to 0.25
- w_query2: bfloat16 [512, 512], replicated, may hold values from -0.25 to 0.25
- w_key2: bfloat16 [512, 512], replicated, may hold values from -0.25 to 0.25
- w_value2: bfloat16 [512, 512], replicated, may hold values from -0.25 to 0.25
- w_out2: bfloat16 [512, 512], replicated, may hold values from -0.25 to 0.25
Outputs:
- updated_field: float32 [64, 64, 16, 512], P('wide', 'narrow')
All inputs are finite; a program needn't handle non-finite values. No bound on the sum of `fluid_mask` on one device may be relied on, other than what follows from the above.
Results may differ from a plain program's by a relative error of at most 0.035.
The roundings to bfloat16 on the way count: a program that leaves them out, or rounds other values in their place, can miss the bound.
Values may be sent and summed in bfloat16 or wider, within the bound.
No kernel may reach another device: no remote copies, remote signals or barrier semaphores. Data moves between devices by JAX's collectives and lax.ppermute only.
A program may use at most 192 MiB of HBM per device.

v0:
```python
import math
import jax
import jax.numpy as jnp
from jax import lax
from jax.sharding import PartitionSpec as P

HEADS = 8


def padded_2(cells, sides, width):
    for axis, dim in sides:
        count = lax.axis_size(axis)
        ends = count - 1
        head = lax.slice_in_dim(cells, 0, width, axis=dim)
        tail = lax.slice_in_dim(cells, cells.shape[dim] - width, cells.shape[dim], axis=dim)
        cells = jnp.concatenate(
            [
                lax.ppermute(tail, axis, [(i, (i + 1) % count) for i in range(ends)]),
                cells,
                lax.ppermute(head, axis, [((i + 1) % count, i) for i in range(ends)]),
            ],
            axis=dim,
        )
    return cells


def head_block(matrix, head_index, head_size):
    return matrix[:, head_index * head_size : (head_index + 1) * head_size]


def pair_scores(queries, key_rows, head_size):
    factor = 1.8 / math.sqrt(head_size)
    return factor * lax.dot_general(
        queries, key_rows, (((1,), (1,)), ((), ())), preferred_element_type=jnp.float32
    )


def project(row_block, weight):
    return jnp.dot(row_block, weight, preferred_element_type=jnp.float32).astype(jnp.bfloat16)


def exact_dot(weights, values_block):
    return jnp.dot(
        weights, values_block, precision=lax.Precision.HIGHEST, preferred_element_type=jnp.float32
    )


def update_state(summed, totals, state_rows, w_out1, head_count):
    row_count, model_width = summed.shape
    shaped = summed.reshape(row_count, head_count, model_width // head_count) / totals[:, :, None]
    read_rows = shaped.reshape(row_count, model_width).astype(jnp.bfloat16)
    updated = state_rows.astype(jnp.float32) + jnp.dot(
        read_rows, w_out1, preferred_element_type=jnp.float32
    )
    return updated.astype(jnp.bfloat16)


def per_device(
    flow_field,
    fluid_mask,
    conv_weight,
    latents,
    w_query1,
    w_key1,
    w_value1,
    w_out1,
    w_query2,
    w_key2,
    w_value2,
    w_out2,
):
    size_x, size_y, size_z, model_width = flow_field.shape
    head_count = HEADS
    head_size = model_width // head_count
    latent_count = latents.shape[0]
    masked = flow_field * fluid_mask[:, :, :, None].astype(jnp.bfloat16)
    padded = padded_2(masked, (("wide", 0), ("narrow", 1)), 1)
    padded = jnp.pad(padded, ((0, 0), (0, 0), (1, 1), (0, 0)))
    stencil = masked.astype(jnp.float32)
    for offset_x in range(3):
        for offset_y in range(3):
            for offset_z in range(3):
                window = padded[
                    offset_x : offset_x + size_x,
                    offset_y : offset_y + size_y,
                    offset_z : offset_z + size_z,
                ]
                stencil = (
                    stencil
                    + window.astype(jnp.float32)
                    * conv_weight[9 * offset_x + 3 * offset_y + offset_z]
                )
    cell_count = size_x * size_y * size_z
    mixed_cells = stencil.astype(jnp.bfloat16).reshape(cell_count, model_width)
    flat_masked = masked.reshape(cell_count, model_width)
    keys1 = project(mixed_cells, w_key1)
    values1 = project(mixed_cells, w_value1)
    values_wide = values1.astype(jnp.float32)
    queries1 = project(latents, w_query1)
    device_count = lax.axis_size("wide") * lax.axis_size("narrow")
    sums_list = []
    totals_list = []
    tops_list = []
    for head_index in range(head_count):
        scores = pair_scores(
            head_block(queries1, head_index, head_size),
            head_block(keys1, head_index, head_size),
            head_size,
        )
        own_top = jnp.max(scores, axis=1, keepdims=True)
        weights = jnp.exp(scores - own_top)
        tops_list.append(own_top[:, 0])
        totals_list.append(jnp.sum(weights, axis=1))
        sums_list.append(exact_dot(weights, head_block(values_wide, head_index, head_size)))
    summed1 = jnp.concatenate(sums_list, axis=1)[None]
    totals1 = jnp.stack(totals_list, axis=1)[None]
    tops1 = jnp.stack(tops_list, axis=1)[None]
    part_sums, part_totals, part_tops = (
        lax.all_to_all(summed1, ("wide", "narrow"), split_axis=1, concat_axis=0, tiled=True),
        lax.all_to_all(totals1, ("wide", "narrow"), split_axis=1, concat_axis=0, tiled=True),
        lax.all_to_all(tops1, ("wide", "narrow"), split_axis=1, concat_axis=0, tiled=True),
    )
    row_count = latent_count // device_count
    largest = jnp.max(part_tops, axis=0, keepdims=True)
    factors = jnp.exp(part_tops - largest)
    totals = jnp.sum(factors * part_totals, axis=0)
    shaped = (
        part_sums.reshape(device_count, row_count, head_count, head_size) * factors[:, :, :, None]
    )
    summed = jnp.sum(shaped, axis=0).reshape(row_count, model_width)
    start = (
        lax.axis_index("wide") * lax.axis_size("narrow") + lax.axis_index("narrow")
    ) * row_count
    own_latents = lax.dynamic_slice_in_dim(latents, start, row_count, 0)
    own_state = update_state(summed, totals, own_latents, w_out1, head_count)
    latent_state = lax.all_gather(own_state, ("wide", "narrow"), axis=0, tiled=True)
    keys2 = project(latent_state, w_key2)
    values2 = project(latent_state, w_value2)
    queries2 = project(mixed_cells, w_query2)
    read_heads = []
    for head_index in range(head_count):
        scores = pair_scores(
            head_block(queries2, head_index, head_size),
            head_block(keys2, head_index, head_size),
            head_size,
        )
        top2 = jnp.max(scores, axis=1, keepdims=True)
        weights = jnp.exp(scores - top2)
        totals = jnp.sum(weights, axis=1, keepdims=True)
        summed = jnp.dot(
            weights.astype(jnp.bfloat16),
            head_block(values2, head_index, head_size),
            preferred_element_type=jnp.float32,
        )
        read_heads.append(summed / totals)
    read2 = jnp.concatenate(read_heads, axis=1).astype(jnp.bfloat16)
    result = flat_masked.astype(jnp.float32) + jnp.dot(
        read2, w_out2, preferred_element_type=jnp.float32
    )
    return result.reshape(size_x, size_y, size_z, model_width)


def solution(mesh):
    return jax.shard_map(
        per_device,
        mesh=mesh,
        in_specs=(
            P("wide", "narrow", None, None),
            P("wide", "narrow", None),
            P(),
            P(),
            P(),
            P(),
            P(),
            P(),
            P(),
            P(),
            P(),
            P(),
        ),
        out_specs=P("wide", "narrow", None, None),
        check_vma=False,
    )
```

profile of v0, /device:TPU:0, one launch (start us, length us, event | category | flops | bytes accessed | tf_op | source)
XLA Modules:
  0.0 399.7 jit_solution(2876258442550393296)
XLA Ops:
  9.5 4.9 %collective-permute-start = (bf16[1,16,16,512]{3,2,1,0:T(8,128)(2,1)S(1)}, bf16[1,16,16,512]{3,2,1,0:T(8,128)(2,1)S(1)}, u32[]{:S(2)}, u32[]{:S(2)}) collective-permute-start(bf16[1,16,16,512]{3,2,1,0:T(8,128)(2,1)S(1)} %get-tuple-element.11), channel_id=1, source_target_pairs={{0,4},{4,8},{8,12},{12,16},{16,20},{20,24},{24,28},{1,5},{5,9},{9,... | collective-permute-start | bytes 786440 | tf_op jit(solution)/shard_map/ppermute | solution.py:18
  16.6 9.0 %collective-permute-done = bf16[1,16,16,512]{3,2,1,0:T(8,128)(2,1)S(1)} collective-permute-done((bf16[1,16,16,512]{3,2,1,0:T(8,128)(2,1)S(1)}, bf16[1,16,16,512]{3,2,1,0:T(8,128)(2,1)S(1)}, u32[]{:S(2)}, u32[]{:S(2)}) %collective-permute-start) | collective-permute-done | bytes 262176 | tf_op jit(solution)/shard_map/ppermute | solution.py:18
  28.3 3.7 collective-permute-done.3
  32.0 2.8 select_maximum_fusion
  35.7 16.4 %add_convert_fusion = bf16[8,16,16,512]{3,2,1,0:T(8,128)(2,1)S(1)} fusion(bf16[8,16,16,512]{3,2,1,0:T(8,128)(2,1)S(1)} %broadcast_multiply_fusion, bf16[10,18,18,512]{3,2,1,0:T(8,128)(2,1)S(1)} %select_maximum_fusion, bf16[10,17,16,512]{3,2,1,0:T(8,128)(2,1)S(1)} %get-tuple-element.8, bf16[1,16,16,512]{3,2,1,0:T(8,128)(2,1)S(1)} %collective-permute-done.1, ...), kind=kLoop, calls=%fused_computation.91 | loop fusion | flops 88080384 | bytes 55105536 | tf_op jit(solution)/shard_map/convert_element_type | solution.py:94
  58.8 4.5 %multiply_reduce_fusion.12 = (f32[1024]{0:T(1024)S(1)}, f32[1024,2048]{1,0:T(8,128)}) fusion(bf16[2048,512]{0,1:T(8,128)(2,1)S(1)} %convolution_convert_fusion.1, bf16[1024,512]{0,1:T(8,128)(2,1)S(1)} %convolution_convert_fusion.5), kind=kOutput, calls=%fused_computation.31 | convolution fusion | flops 272628736 | bytes 8785920 | tf_op jit(solution)/shard_map/dot_general | solution.py:33
  63.3 4.5 %multiply_reduce_fusion.13 = (f32[1024]{0:T(1024)S(1)}, f32[1024,2048]{1,0:T(8,128)}) fusion(bf16[2048,512]{0,1:T(8,128)(2,1)S(1)} %convolution_convert_fusion.1, bf16[1024,512]{0,1:T(8,128)(2,1)S(1)} %convolution_convert_fusion.5), kind=kOutput, calls=%fused_computation.32 | convolution fusion | flops 272628736 | bytes 8785920 | tf_op jit(solution)/shard_map/dot_general | solution.py:33
  67.8 4.5 %multiply_reduce_fusion.14 = (f32[1024]{0:T(1024)S(1)}, f32[1024,2048]{1,0:T(8,128)}) fusion(bf16[2048,512]{0,1:T(8,128)(2,1)S(1)} %convolution_convert_fusion.1, bf16[1024,512]{0,1:T(8,128)(2,1)S(1)} %convolution_convert_fusion.5), kind=kOutput, calls=%fused_computation.33 | convolution fusion | flops 272628736 | bytes 8785920 | tf_op jit(solution)/shard_map/dot_general | solution.py:33
  72.3 4.5 %multiply_reduce_fusion.15 = (f32[1024]{0:T(1024)S(1)}, f32[1024,2048]{1,0:T(8,128)}) fusion(bf16[2048,512]{0,1:T(8,128)(2,1)S(1)} %convolution_convert_fusion.1, bf16[1024,512]{0,1:T(8,128)(2,1)S(1)} %convolution_convert_fusion.5), kind=kOutput, calls=%fused_computation.34 | convolution fusion | flops 272628736 | bytes 8785920 | tf_op jit(solution)/shard_map/dot_general | solution.py:33
  76.8 2.8 convolution_convert_fusion
  79.6 4.4 %fusion.1 = f32[1024]{0:T(1024)S(1)} fusion(f32[1024,2048]{1,0:T(8,128)} %get-tuple-element.41, f32[1024]{0:T(1024)S(1)} %get-tuple-element.40), kind=kLoop, calls=%fused_computation.35 | loop fusion | flops 6290432 | bytes 8396800 | tf_op jit(solution)/shard_map/reduce_sum | solution.py:113
  83.9 7.9 %fusion.149 = f32[1024,512]{0,1:T(8,128)S(1)} fusion(f32[1024,2048]{1,0:T(8,128)} %get-tuple-element.41, f32[1024]{0:T(1024)S(1)} %get-tuple-element.40, bf16[2048,512]{0,1:T(8,128)(2,1)} %convolution_convert_fusion), kind=kOutput, calls=%fused_computation.142 | convolution fusion | flops 1614807040 | bytes 8916992 | tf_op jit(solution)/shard_map/dot_general | solution.py:43
  91.8 4.4 %fusion.3 = f32[1024]{0:T(1024)S(1)} fusion(f32[1024,2048]{1,0:T(8,128)} %get-tuple-element.43, f32[1024]{0:T(1024)S(1)} %get-tuple-element.42), kind=kLoop, calls=%fused_computation.37 | loop fusion | flops 6290432 | bytes 8396800 | tf_op jit(solution)/shard_map/reduce_sum | solution.py:113
  96.2 8.1 %fusion.148 = f32[1024,512]{0,1:T(8,128)S(1)} fusion(f32[1024,512]{0,1:T(8,128)S(1)} %fusion.149, f32[1024,2048]{1,0:T(8,128)} %get-tuple-element.43, f32[1024]{0:T(1024)S(1)} %get-tuple-element.42, bf16[2048,512]{0,1:T(8,128)(2,1)} %convolution_convert_fusion), kind=kOutput, calls=%fused_computation.141 | convolution fusion | flops 1614807040 | bytes 8916992 | tf_op jit(solution)/shard_map/dot_general | solution.py:43
  104.3 4.4 %fusion.5 = f32[1024]{0:T(1024)S(1)} fusion(f32[1024,2048]{1,0:T(8,128)} %get-tuple-element.45, f32[1024]{0:T(1024)S(1)} %get-tuple-element.44), kind=kLoop, calls=%fused_computation.39 | loop fusion | flops 6290432 | bytes 8396800 | tf_op jit(solution)/shard_map/reduce_sum | solution.py:113
  108.7 8.1 %fusion.147 = f32[1024,512]{0,1:T(8,128)S(1)} fusion(f32[1024,512]{0,1:T(8,128)S(1)} %fusion.148, f32[1024,2048]{1,0:T(8,128)} %get-tuple-element.45, f32[1024]{0:T(1024)S(1)} %get-tuple-element.44, bf16[2048,512]{0,1:T(8,128)(2,1)} %convolution_convert_fusion), kind=kOutput, calls=%fused_computation.140 | convolution fusion | flops 1614807040 | bytes 8916992 | tf_op jit(solution)/shard_map/dot_general | solution.py:43
  116.8 4.4 %fusion.7 = f32[1024]{0:T(1024)S(1)} fusion(f32[1024,2048]{1,0:T(8,128)} %get-tuple-element.47, f32[1024]{0:T(1024)S(1)} %get-tuple-element.46), kind=kLoop, calls=%fused_computation.41 | loop fusion | flops 6290432 | bytes 8396800 | tf_op jit(solution)/shard_map/reduce_sum | solution.py:113
  121.1 8.3 %fusion.146 = f32[1024,512]{0,1:T(8,128)S(1)} fusion(f32[1024,512]{0,1:T(8,128)S(1)} %fusion.147, f32[1024,2048]{1,0:T(8,128)} %get-tuple-element.47, f32[1024]{0:T(1024)S(1)} %get-tuple-element.46, bf16[2048,512]{0,1:T(8,128)(2,1)} %convolution_convert_fusion), kind=kOutput, calls=%fused_computation.139 | convolution fusion | flops 1614807040 | bytes 8916992 | tf_op jit(solution)/shard_map/dot_general | solution.py:43
  131.4 6.5 %fusion.145 = f32[1024,512]{0,1:T(8,128)S(1)} fusion(f32[1024,512]{0,1:T(8,128)S(1)} %fusion.146, f32[1024,2048]{1,0:T(8,128)S(1)} %get-tuple-element.49, f32[1024]{0:T(1024)S(1)} %get-tuple-element.48, bf16[2048,512]{0,1:T(8,128)(2,1)} %convolution_convert_fusion), kind=kOutput, calls=%fused_computation.138 | convolution fusion | flops 1614807040 | bytes 8916992 | tf_op jit(solution)/shard_map/dot_general | solution.py:43
  137.9 2.3 fusion.11
  140.2 6.5 %fusion.144 = f32[1024,512]{0,1:T(8,128)S(1)} fusion(f32[1024,512]{0,1:T(8,128)S(1)} %fusion.145, f32[1024,2048]{1,0:T(8,128)S(1)} %get-tuple-element.51, f32[1024]{0:T(1024)S(1)} %get-tuple-element.50, bf16[2048,512]{0,1:T(8,128)(2,1)} %convolution_convert_fusion), kind=kOutput, calls=%fused_computation.137 | convolution fusion | flops 1614807040 | bytes 8916992 | tf_op jit(solution)/shard_map/dot_general | solution.py:43
  154.3 9.5 %all-to-all-start.1 = ((f32[32,1,256]{2,1,0:T(1,128)}), f32[32,1,256]{2,1,0:T(1,128)S(1)}, u32[]{:S(2)}, u32[]{:S(2)}) async-start(f32[32,1,256]{2,1,0:T(1,128)} %reshape.112), calls=%async_computation.1 | async-start | bytes 65536 | tf_op jit(solution)/shard_map/all_to_all | solution.py:121
  163.8 8.1 %fusion.143 = f32[1024,512]{0,1:T(8,128)S(1)} fusion(f32[1024,512]{0,1:T(8,128)S(1)} %fusion.144, f32[1024,2048]{1,0:T(8,128)} %copy-done.3, f32[1024]{0:T(1024)S(1)} %get-tuple-element.52, bf16[2048,512]{0,1:T(8,128)(2,1)} %convolution_convert_fusion), kind=kOutput, calls=%fused_computation.136 | convolution fusion | flops 1614807040 | bytes 8916992 | tf_op jit(solution)/shard_map/dot_general | solution.py:43
  175.1 5.9 %all-to-all-start.2 = ((f32[32,1,256]{2,1,0:T(1,128)}), f32[32,1,256]{2,1,0:T(1,128)S(1)}, u32[]{:S(2)}, u32[]{:S(2)}) async-start(f32[32,1,256]{2,1,0:T(1,128)} %reshape.114), calls=%async_computation.2 | async-start | bytes 65536 | tf_op jit(solution)/shard_map/all_to_all | solution.py:120
  181.1 8.1 %fusion.142 = f32[1024,512]{0,1:T(8,128)S(1)} fusion(f32[1024,512]{0,1:T(8,128)S(1)} %fusion.143, f32[1024,2048]{1,0:T(8,128)} %copy-done.2, f32[1024]{0:T(1024)S(1)} %get-tuple-element.54, bf16[2048,512]{0,1:T(8,128)(2,1)} %convolution_convert_fusion), kind=kOutput, calls=%fused_computation.135 | convolution fusion | flops 1614807040 | bytes 8916992 | tf_op jit(solution)/shard_map/dot_general | solution.py:43
  189.2 3.7 copy.23
  192.9 6.0 %all-to-all-start = ((f32[1,1024,512]{2,0,1:T(1,128)}), f32[1,1024,512]{2,0,1:T(1,128)}, u32[]{:S(2)}, u32[]{:S(2)}) async-start(f32[1,1024,512]{2,0,1:T(1,128)} %copy.23), calls=%async_computation | async-start | bytes 4194304 | tf_op jit(solution)/shard_map/all_to_all | solution.py:119
  203.2 2.6 mul.451
  205.8 3.6 mul.452
  209.5 38.1 %all-to-all-done = f32[1,1024,512]{2,0,1:T(1,128)} async-done(((f32[1,1024,512]{2,0,1:T(1,128)}), f32[1,1024,512]{2,0,1:T(1,128)}, u32[]{:S(2)}, u32[]{:S(2)}) %all-to-all-start) | async-done | bytes 2097184 | tf_op jit(solution)/shard_map/all_to_all | solution.py:119
  251.4 2.9 convolution_convert_fusion.2
  254.4 50.3 %all-gather.2.cloned.1.call-done = bf16[1024,512]{1,0:T(8,128)(2,1)} async-done(((bf16[32,512]{1,0:T(8,128)(2,1)}), bf16[1024,512]{1,0:T(8,128)(2,1)}) %all-gather.2.cloned.1.call-update) | async-done | bytes 1048592 | tf_op jit(solution)/shard_map/all_gather | solution.py:136
  304.7 2.0 convolution_convert_fusion.4
  310.6 4.5 %multiply_reduce_fusion.3 = (f32[2048]{0:T(1024)S(1)}, f32[2048,1024]{0,1:T(8,128)}) fusion(bf16[1024,512]{0,1:T(8,128)(2,1)S(1)} %convolution_convert_fusion.4, bf16[2048,512]{0,1:T(8,128)(2,1)S(1)} %convolution_convert_fusion.2), kind=kOutput, calls=%fused_computation.22 | convolution fusion | flops 272627712 | bytes 8790016 | tf_op jit(solution)/shard_map/dot_general | solution.py:33
  315.1 4.5 %multiply_reduce_fusion.4 = (f32[2048]{0:T(1024)S(1)}, f32[2048,1024]{0,1:T(8,128)}) fusion(bf16[1024,512]{0,1:T(8,128)(2,1)S(1)} %convolution_convert_fusion.4, bf16[2048,512]{0,1:T(8,128)(2,1)S(1)} %convolution_convert_fusion.2), kind=kOutput, calls=%fused_computation.23 | convolution fusion | flops 272627712 | bytes 8790016 | tf_op jit(solution)/shard_map/dot_general | solution.py:33
  319.6 4.5 %multiply_reduce_fusion.5 = (f32[2048]{0:T(1024)S(1)}, f32[2048,1024]{0,1:T(8,128)}) fusion(bf16[1024,512]{0,1:T(8,128)(2,1)S(1)} %convolution_convert_fusion.4, bf16[2048,512]{0,1:T(8,128)(2,1)S(1)} %convolution_convert_fusion.2), kind=kOutput, calls=%fused_computation.24 | convolution fusion | flops 272627712 | bytes 8790016 | tf_op jit(solution)/shard_map/dot_general | solution.py:33
  324.2 4.5 %multiply_reduce_fusion.6 = (f32[2048]{0:T(1024)S(1)}, f32[2048,1024]{0,1:T(8,128)}) fusion(bf16[1024,512]{0,1:T(8,128)(2,1)S(1)} %convolution_convert_fusion.4, bf16[2048,512]{0,1:T(8,128)(2,1)S(1)} %convolution_convert_fusion.2), kind=kOutput, calls=%fused_computation.25 | convolution fusion | flops 272627712 | bytes 8790016 | tf_op jit(solution)/shard_map/dot_general | solution.py:33
  328.7 5.0 %multiply_reduce_fusion.7 = (f32[2048]{0:T(1024)S(1)}, f32[2048,1024]{0,1:T(8,128)}) fusion(bf16[1024,512]{0,1:T(8,128)(2,1)S(1)} %convolution_convert_fusion.4, bf16[2048,512]{0,1:T(8,128)(2,1)S(1)} %convolution_convert_fusion.2), kind=kOutput, calls=%fused_computation.26 | convolution fusion | flops 272627712 | bytes 8790016 | tf_op jit(solution)/shard_map/dot_general | solution.py:33
  337.9 4.8 %fusion.25 = f32[2048]{0:T(1024)S(1)} fusion(f32[2048,1024]{0,1:T(8,128)} %get-tuple-element.65, f32[2048]{0:T(1024)S(1)} %get-tuple-element.64), kind=kLoop, calls=%fused_computation.59 | loop fusion | flops 6289408 | bytes 8404992 | tf_op jit(solution)/shard_map/reduce_sum | solution.py:149
  342.7 4.8 %fusion.23 = f32[2048]{0:T(1024)S(1)} fusion(f32[2048,1024]{0,1:T(8,128)} %get-tuple-element.63, f32[2048]{0:T(1024)S(1)} %get-tuple-element.62), kind=kLoop, calls=%fused_computation.57 | loop fusion | flops 6289408 | bytes 8404992 | tf_op jit(solution)/shard_map/reduce_sum | solution.py:149
  347.4 4.8 %fusion.21 = f32[2048]{0:T(1024)S(1)} fusion(f32[2048,1024]{0,1:T(8,128)} %get-tuple-element.61, f32[2048]{0:T(1024)S(1)} %get-tuple-element.60), kind=kLoop, calls=%fused_computation.55 | loop fusion | flops 6289408 | bytes 8404992 | tf_op jit(solution)/shard_map/reduce_sum | solution.py:149
  352.2 4.8 %fusion.19 = f32[2048]{0:T(1024)S(1)} fusion(f32[2048,1024]{0,1:T(8,128)} %get-tuple-element.59, f32[2048]{0:T(1024)S(1)} %get-tuple-element.58), kind=kLoop, calls=%fused_computation.53 | loop fusion | flops 6289408 | bytes 8404992 | tf_op jit(solution)/shard_map/reduce_sum | solution.py:149
  357.0 5.1 %fusion.17 = f32[2048]{0:T(1024)S(1)} fusion(f32[2048,1024]{0,1:T(8,128)} %get-tuple-element.57, f32[2048]{0:T(1024)S(1)} %get-tuple-element.56), kind=kLoop, calls=%fused_computation.51 | loop fusion | flops 6289408 | bytes 8404992 | tf_op jit(solution)/shard_map/reduce_sum | solution.py:149
  362.9 4.9 %fusion.76 = bf16[2048,512]{0,1:T(8,128)(2,1)S(1)} fusion(f32[2048,1024]{0,1:T(8,128)} %get-tuple-element.57, f32[2048]{0:T(1024)S(1)} %get-tuple-element.56, f32[2048]{0:T(1024)S(1)} %fusion.17, bf16[1024,512]{0,1:T(8,128)(2,1)S(1)} %convolution_convert_fusion.3), kind=kOutput, calls=%fused_computation.107 | convolution fusion | flops 274989056 | bytes 8798208 | tf_op jit(solution)/shard_map/dot_general | solution.py:150
  367.8 4.9 %fusion.85 = bf16[2048,512]{0,1:T(8,128)(2,1)S(1)} fusion(bf16[2048,512]{0,1:T(8,128)(2,1)S(1)} %fusion.76, f32[2048,1024]{0,1:T(8,128)} %get-tuple-element.59, f32[2048]{0:T(1024)S(1)} %get-tuple-element.58, f32[2048]{0:T(1024)S(1)} %fusion.19, bf16[1024,512]{0,1:T(8,128)(2,1)S(1)} %convolution_convert_fusion.3), kind=kOutput, calls=%fused_computation.110 | convolution fusion | flops 274989056 | bytes 8798208 | tf_op jit(solution)/shard_map/dot_general | solution.py:150
  372.8 5.1 %fusion.94 = bf16[2048,512]{0,1:T(8,128)(2,1)S(1)} fusion(bf16[2048,512]{0,1:T(8,128)(2,1)S(1)} %fusion.85, f32[2048,1024]{0,1:T(8,128)} %get-tuple-element.61, f32[2048]{0:T(1024)S(1)} %get-tuple-element.60, f32[2048]{0:T(1024)S(1)} %fusion.21, bf16[1024,512]{0,1:T(8,128)(2,1)S(1)} %convolution_convert_fusion.3), kind=kOutput, calls=%fused_computation.113 | convolution fusion | flops 274989056 | bytes 8798208 | tf_op jit(solution)/shard_map/dot_general | solution.py:150
  377.8 5.1 %fusion.103 = bf16[2048,512]{0,1:T(8,128)(2,1)S(1)} fusion(bf16[2048,512]{0,1:T(8,128)(2,1)S(1)} %fusion.94, f32[2048,1024]{0,1:T(8,128)} %get-tuple-element.63, f32[2048]{0:T(1024)S(1)} %get-tuple-element.62, f32[2048]{0:T(1024)S(1)} %fusion.23, bf16[1024,512]{0,1:T(8,128)(2,1)S(1)} %convolution_convert_fusion.3), kind=kOutput, calls=%fused_computation.116 | convolution fusion | flops 274989056 | bytes 8798208 | tf_op jit(solution)/shard_map/dot_general | solution.py:150
  389.3 3.3 bitcast_add_fusion
  (100 shorter events, 51.4 us)
Async XLA Ops:
  6.5 45.5 %copy-start = (bf16[512,512]{1,0:T(8,128)(2,1)S(1)}, bf16[512,512]{1,0:T(8,128)(2,1)}, u32[]{:S(2)}) copy-start(bf16[512,512]{1,0:T(8,128)(2,1)} %param.17) | copy-start | bytes 1572868
  6.5 9.2 %copy-start.9 = (f32[27,512]{1,0:T(8,128)S(1)}, f32[27,512]{1,0:T(8,128)}, u32[]{:S(2)}) copy-start(f32[27,512]{1,0:T(8,128)} %param.14) | copy-start | bytes 165892
  6.5 9.2 %copy-start.10 = (bf16[1024,512]{1,0:T(8,128)(2,1)S(1)}, bf16[1024,512]{1,0:T(8,128)(2,1)}, u32[]{:S(2)}) copy-start(bf16[1024,512]{1,0:T(8,128)(2,1)} %param.15) | copy-start | bytes 3145732
  6.5 9.2 %copy-start.12 = (bf16[512,512]{1,0:T(8,128)(2,1)S(1)}, bf16[512,512]{1,0:T(8,128)(2,1)}, u32[]{:S(2)}) copy-start(bf16[512,512]{1,0:T(8,128)(2,1)} %param.16) | copy-start | bytes 1572868
  9.5 26.2 %copy-start.4 = (bf16[8,16,16,512]{3,2,1,0:T(8,128)(2,1)}, bf16[8,16,16,512]{3,2,1,0:T(8,128)(2,1)S(1)}, u32[]{:S(2)}) copy-start(bf16[8,16,16,512]{3,2,1,0:T(8,128)(2,1)S(1)} %broadcast_multiply_fusion) | copy-start | bytes 6291460
  9.5 16.0 %collective-permute-start = (bf16[1,16,16,512]{3,2,1,0:T(8,128)(2,1)S(1)}, bf16[1,16,16,512]{3,2,1,0:T(8,128)(2,1)S(1)}, u32[]{:S(2)}, u32[]{:S(2)}) collective-permute-start(bf16[1,16,16,512]{3,2,1,0:T(8,128)(2,1)S(1)} %get-tuple-element.11), channel_id=1, source_target_pairs={{0,4},{4,8},{8,12},{12,16},{16,20},{20,24},{24,28},{1,5},{5,9},{9,... | collective-permute-start | bytes 786440 | tf_op jit(solution)/shard_map/ppermute | solution.py:18
  14.4 11.2 %collective-permute-start.1 = (bf16[1,16,16,512]{3,2,1,0:T(8,128)(2,1)S(1)}, bf16[1,16,16,512]{3,2,1,0:T(8,128)(2,1)S(1)}, u32[]{:S(2)}, u32[]{:S(2)}) collective-permute-start(bf16[1,16,16,512]{3,2,1,0:T(8,128)(2,1)S(1)} %get-tuple-element.12), channel_id=1, source_target_pairs={{4,0},{8,4},{12,8},{16,12},{20,16},{24,20},{28,24},{5,1},{9,5},{13... | collective-permute-start | bytes 786440 | tf_op jit(solution)/shard_map/ppermute | solution.py:20
  25.6 2.6 collective-permute-start.2
  26.9 5.0 %collective-permute-start.3 = (bf16[10,1,16,512]{3,2,1,0:T(8,128)(2,1)S(1)}, bf16[10,1,16,512]{3,2,1,0:T(8,128)(2,1)S(1)}, u32[]{:S(2)}, u32[]{:S(2)}) collective-permute-start(bf16[10,1,16,512]{3,2,1,0:T(8,128)(2,1)S(1)} %get-tuple-element.10), channel_id=1, source_target_pairs={{1,0},{2,1},{3,2},{5,4},{6,5},{7,6},{9,8},{10,9},{11,10},{13,12},{... | collective-permute-start | bytes 491528 | tf_op jit(solution)/shard_map/ppermute | solution.py:20
  52.1 24.7 %copy-start.6 = (bf16[8,16,16,512]{3,2,1,0:T(8,128)(2,1)}, bf16[8,16,16,512]{3,2,1,0:T(8,128)(2,1)S(1)}, u32[]{:S(2)}) copy-start(bf16[8,16,16,512]{3,2,1,0:T(8,128)(2,1)S(1)} %add_convert_fusion) | copy-start | bytes 6291460
  54.7 92.0 %copy-start.2 = (f32[1024,2048]{1,0:T(8,128)}, f32[1024,2048]{1,0:T(8,128)S(1)}, u32[]{:S(2)}) copy-start(f32[1024,2048]{1,0:T(8,128)S(1)} %get-tuple-element.55) | copy-start | bytes 25165828
  56.1 92.5 %copy-start.3 = (f32[1024,2048]{1,0:T(8,128)}, f32[1024,2048]{1,0:T(8,128)S(1)}, u32[]{:S(2)}) copy-start(f32[1024,2048]{1,0:T(8,128)S(1)} %get-tuple-element.53) | copy-start | bytes 25165828
  72.3 4.5 %copy-start.13 = (bf16[512,512]{1,0:T(8,128)(2,1)S(1)}, bf16[512,512]{1,0:T(8,128)(2,1)}, u32[]{:S(2)}) copy-start(bf16[512,512]{1,0:T(8,128)(2,1)} %param.18) | copy-start | bytes 1572868
  154.3 20.8 %all-to-all-start.1 = ((f32[32,1,256]{2,1,0:T(1,128)}), f32[32,1,256]{2,1,0:T(1,128)S(1)}, u32[]{:S(2)}, u32[]{:S(2)}) async-start(f32[32,1,256]{2,1,0:T(1,128)} %reshape.112), calls=%async_computation.1 | async-start | bytes 65536 | tf_op jit(solution)/shard_map/all_to_all | solution.py:121
  175.1 17.8 %all-to-all-start.2 = ((f32[32,1,256]{2,1,0:T(1,128)}), f32[32,1,256]{2,1,0:T(1,128)S(1)}, u32[]{:S(2)}, u32[]{:S(2)}) async-start(f32[32,1,256]{2,1,0:T(1,128)} %reshape.114), calls=%async_computation.2 | async-start | bytes 65536 | tf_op jit(solution)/shard_map/all_to_all | solution.py:120
  192.9 54.7 %all-to-all-start = ((f32[1,1024,512]{2,0,1:T(1,128)}), f32[1,1024,512]{2,0,1:T(1,128)}, u32[]{:S(2)}, u32[]{:S(2)}) async-start(f32[1,1024,512]{2,0,1:T(1,128)} %copy.23), calls=%async_computation | async-start | bytes 4194304 | tf_op jit(solution)/shard_map/all_to_all | solution.py:119
  198.9 105.8 %all-gather.2.cloned.1.call-start = ((), (), s32[]{:S(2)}) async-start(), calls=%async_computation.3 | async-start | bytes 1081344 | tf_op jit(solution)/shard_map/all_gather | solution.py:136
  209.4 40.4 %copy-start.8 = (bf16[512,512]{1,0:T(8,128)(2,1)S(1)}, bf16[512,512]{1,0:T(8,128)(2,1)}, u32[]{:S(2)}) copy-start(bf16[512,512]{1,0:T(8,128)(2,1)} %param.19) | copy-start | bytes 1572868
  209.5 42.0 %copy-start.14 = (bf16[512,512]{1,0:T(8,128)(2,1)S(1)}, bf16[512,512]{1,0:T(8,128)(2,1)}, u32[]{:S(2)}) copy-start(bf16[512,512]{1,0:T(8,128)(2,1)} %param.20) | copy-start | bytes 1572868
  251.4 53.2 %copy-start.15 = (bf16[512,512]{1,0:T(8,128)(2,1)S(1)}, bf16[512,512]{1,0:T(8,128)(2,1)}, u32[]{:S(2)}) copy-start(bf16[512,512]{1,0:T(8,128)(2,1)} %param.21) | copy-start | bytes 1572868
  357.0 5.1 %copy-start.11 = (bf16[1024,512]{1,0:T(8,128)(2,1)S(1)}, bf16[1024,512]{1,0:T(8,128)(2,1)}, u32[]{:S(2)}) copy-start(bf16[1024,512]{1,0:T(8,128)(2,1)} %all-gather.2.cloned.1.call-done) | copy-start | bytes 3145732
  357.0 5.1 %copy-start.16 = (bf16[512,512]{1,0:T(8,128)(2,1)S(1)}, bf16[512,512]{1,0:T(8,128)(2,1)}, u32[]{:S(2)}) copy-start(bf16[512,512]{1,0:T(8,128)(2,1)} %param.22) | copy-start | bytes 1572868
  372.7 10.2 %slice-start = ((s8[8388608]{0:T(1024)(128)(4,1)}), s8[4194304]{0:T(1024)(128)(4,1)S(1)}, s32[]{:S(2)}) async-start(s8[8388608]{0:T(1024)(128)(4,1)} %bitcast.74), calls=%async_computation.4 | async-start | bytes 8388608
  377.8 5.1 %slice-start.1 = ((s8[8388608]{0:T(1024)(128)(4,1)}), s8[4194304]{0:T(1024)(128)(4,1)S(1)}, s32[]{:S(2)}) async-start(s8[8388608]{0:T(1024)(128)(4,1)} %bitcast.74), calls=%async_computation.5 | async-start | bytes 8388608
  387.6 1.6 copy-start.5
  387.6 1.7 copy-start.7
  387.6 5.0 %copy-start.1 = (bf16[512,512]{1,0:T(8,128)(2,1)S(1)}, bf16[512,512]{1,0:T(8,128)(2,1)}, u32[]{:S(2)}) copy-start(bf16[512,512]{1,0:T(8,128)(2,1)} %param.17) | copy-start | bytes 1572868
Sparse Core Ops, SparseCore 0:
  251.5 53.0 all-gather.1
where the time goes:
time: 405 us; the launch traced here: 400 us
  matrix products  154 us (38%)
  waiting for transfers between devices  101 us (25%)
  other arithmetic  82.8 us (20%)
  starting transfers between devices  30.2 us (7%)
  local copies, waits for them, and re-layouts  17.8 us (4%)
  between operations  14.2 us (4%)
    dot_general x8, matrix products, exact_dot(): jnp.dot(weights, values_block, precision=lax.Precision.HIGHEST, preferred...  61.6 us
    dot_general x16, matrix products, pair_scores(): lax.dot_general(queries, key_rows, (((1,), (1,)), ((), ())), preferred_el...  50.3 us
    all_gather x1, waiting for transfers between devices, per_device(): lax.all_gather(own_state, ('wide', 'narrow'), axis=0, tiled=True)  50.3 us
    all_to_all x1, waiting for transfers between devices, per_device(): lax.all_to_all(summed1, ('wide', 'narrow'), split_axis=1, concat_axis=0,...  38.1 us
    reduce_sum x8, other arithmetic, per_device(): totals = jnp.sum(weights, axis=1, keepdims=True)  28.4 us
    dot_general x8, matrix products, per_device(): jnp.dot(weights.astype(jnp.bfloat16), head_block(values2, head_index, hea...  26.2 us
    reduce_sum x8, other arithmetic, per_device(): totals_list.append(jnp.sum(weights, axis=1))  25.6 us
    convert_element_type x1, other arithmetic, per_device(): mixed_cells = stencil.astype(jnp.bfloat16).reshape(cell_count, model_width)  16.4 us
  transfers between devices with their start and end apart: 8, of which 4 were waited for; matrix products, arithmetic and copies ran while one was open for 9% of the time, Pallas kernels for 0%

commit v1 on v0

--- a/solution.py
+++ b/solution.py
@@ -116,7 +116,15 @@
     totals1 = jnp.stack(totals_list, axis=1)[None]
     tops1 = jnp.stack(tops_list, axis=1)[None]
     part_sums, part_totals, part_tops = (
-        lax.all_to_all(summed1, ("wide", "narrow"), split_axis=1, concat_axis=0, tiled=True),
+        jnp.concatenate(
+            lax.all_to_all(
+                jnp.stack(jnp.split(summed1, lax.axis_size(("wide", "narrow")), axis=1)),
+                ("wide", "narrow"),
+                0,
+                0,
+            ),
+            axis=0,
+        ),
         lax.all_to_all(totals1, ("wide", "narrow"), split_axis=1, concat_axis=0, tiled=True),
         lax.all_to_all(tops1, ("wide", "narrow"), split_axis=1, concat_axis=0, tiled=True),
     )

time: 405 us -> 460 us (1.14)
  local copies, waits for them, and re-layouts: 17.8 us -> 73.4 us
  matrix products: 154 us -> 146 us
  waiting for transfers between devices: 101 us -> 107 us
    another operation x0 -> x35, local copies, waits for them, and re-layouts: none -> 34.9 us  [per_device(): jnp.stack(jnp.split(summed1, lax.axis_size(('wide', 'narrow')), axis=1))]
    unnamed x44 -> x76, local copies, waits for them, and re-layouts: 5.99 us -> 30.5 us
    dot_general x8, matrix products: 61.6 us -> 54.4 us  [exact_dot(): jnp.dot(weights, values_block, precision=lax.Precision.HIGHEST, preferred...]
    all_to_all x1, waiting for transfers between devices: 0.01 us -> 6.62 us  [per_device(): lax.all_to_all(totals1, ('wide', 'narrow'), split_axis=1, concat_axis=0,...]
  transfers between devices with their start and end apart: 8 -> 8, of which waited for: 4 -> 5; matrix products, arithmetic and copies ran while one was open for 9% -> 16% of each run, Pallas kernels for 0% -> 0%
where the time goes in v1:
time: 460 us; the launch traced here: 454 us
  matrix products  146 us (32%)
  waiting for transfers between devices  107 us (23%)
  other arithmetic  85.7 us (19%)
  local copies, waits for them, and re-layouts  73.4 us (16%)
  starting transfers between devices  27.9 us (6%)
  between operations  14.2 us (3%)
    dot_general x8, matrix products, exact_dot(): jnp.dot(weights, values_block, precision=lax.Precision.HIGHEST, preferred...  54.4 us
    all_gather x1, waiting for transfers between devices, per_device(): lax.all_gather(own_state, ('wide', 'narrow'), axis=0, tiled=True)  50.1 us
    dot_general x16, matrix products, pair_scores(): lax.dot_general(queries, key_rows, (((1,), (1,)), ((), ())), preferred_el...  50.1 us
    all_to_all x1, waiting for transfers between devices, per_device(): lax.all_to_all(jnp.stack(jnp.split(summed1, lax.axis_size(('wide', 'narro...  37.2 us
    another operation x35, local copies, waits for them, and re-layouts, per_device(): jnp.stack(jnp.split(summed1, lax.axis_size(('wide', 'narrow')), axis=1))  34.9 us
    unnamed x76, local copies, waits for them, and re-layouts  30.5 us
    reduce_sum x8, other arithmetic, per_device(): totals = jnp.sum(weights, axis=1, keepdims=True)  28.5 us
    dot_general x8, matrix products, per_device(): jnp.dot(weights.astype(jnp.bfloat16), head_block(values2, head_index, hea...  26.2 us
  transfers between devices with their start and end apart: 8, of which 5 were waited for; matrix products, arithmetic and copies ran while one was open for 16% of the time, Pallas kernels for 0%

profile of v1, /device:TPU:0, one launch (start us, length us, event | category | flops | bytes accessed | tf_op | source)
XLA Modules:
  0.0 454.2 jit_solution(10307164598530181682)
XLA Ops:
  9.5 4.9 %collective-permute-start = (bf16[1,16,16,512]{3,2,1,0:T(8,128)(2,1)S(1)}, bf16[1,16,16,512]{3,2,1,0:T(8,128)(2,1)S(1)}, u32[]{:S(2)}, u32[]{:S(2)}) collective-permute-start(bf16[1,16,16,512]{3,2,1,0:T(8,128)(2,1)S(1)} %get-tuple-element.43), channel_id=1, source_target_pairs={{0,4},{4,8},{8,12},{12,16},{16,20},{20,24},{24,28},{1,5},{5,9},{9,... | collective-permute-start | bytes 786440 | tf_op jit(solution)/shard_map/ppermute | solution.py:18
  16.6 9.0 %collective-permute-done = bf16[1,16,16,512]{3,2,1,0:T(8,128)(2,1)S(1)} collective-permute-done((bf16[1,16,16,512]{3,2,1,0:T(8,128)(2,1)S(1)}, bf16[1,16,16,512]{3,2,1,0:T(8,128)(2,1)S(1)}, u32[]{:S(2)}, u32[]{:S(2)}) %collective-permute-start) | collective-permute-done | bytes 262176 | tf_op jit(solution)/shard_map/ppermute | solution.py:18
  28.3 3.7 collective-permute-done.3
  32.0 2.8 select_maximum_fusion
  35.7 16.4 %add_convert_fusion = bf16[8,16,16,512]{3,2,1,0:T(8,128)(2,1)S(1)} fusion(bf16[8,16,16,512]{3,2,1,0:T(8,128)(2,1)S(1)} %broadcast_multiply_fusion, bf16[10,18,18,512]{3,2,1,0:T(8,128)(2,1)S(1)} %select_maximum_fusion, bf16[10,17,16,512]{3,2,1,0:T(8,128)(2,1)S(1)} %get-tuple-element.8, bf16[1,16,16,512]{3,2,1,0:T(8,128)(2,1)S(1)} %collective-permute-done.1, ...), kind=kLoop, calls=%fused_computation.91 | loop fusion | flops 88080384 | bytes 55105536 | tf_op jit(solution)/shard_map/convert_element_type | solution.py:94
  58.8 4.5 multiply_reduce_fusion.12
  63.3 4.5 multiply_reduce_fusion.13
  67.8 4.5 multiply_reduce_fusion.14
  72.3 4.5 multiply_reduce_fusion.15
  76.8 2.8 convolution_convert_fusion
  79.6 4.5 fusion.1
  84.1 7.8 %fusion.149 = f32[1024,512]{0,1:T(8,128)S(1)} fusion(f32[1024,2048]{1,0:T(8,128)} %get-tuple-element.73, f32[1024]{0:T(1024)S(1)} %get-tuple-element.72, bf16[2048,512]{0,1:T(8,128)(2,1)S(1)} %copy-done.5), kind=kOutput, calls=%fused_computation.142 | convolution fusion | flops 1614807040 | bytes 8916992 | tf_op jit(solution)/shard_map/dot_general | solution.py:43
  92.0 4.4 fusion.3
  96.3 8.1 %fusion.148 = f32[1024,512]{0,1:T(8,128)S(1)} fusion(f32[1024,512]{0,1:T(8,128)S(1)} %fusion.149, f32[1024,2048]{1,0:T(8,128)} %get-tuple-element.75, f32[1024]{0:T(1024)S(1)} %get-tuple-element.74, bf16[2048,512]{0,1:T(8,128)(2,1)S(1)} %copy-done.5), kind=kOutput, calls=%fused_computation.141 | convolution fusion | flops 1614807040 | bytes 8916992 | tf_op jit(solution)/shard_map/dot_general | solution.py:43
  104.4 4.4 fusion.5
  108.8 8.1 %fusion.147 = f32[1024,512]{0,1:T(8,128)S(1)} fusion(f32[1024,512]{0,1:T(8,128)S(1)} %fusion.148, f32[1024,2048]{1,0:T(8,128)} %get-tuple-element.77, f32[1024]{0:T(1024)S(1)} %get-tuple-element.76, bf16[2048,512]{0,1:T(8,128)(2,1)S(1)} %copy-done.5), kind=kOutput, calls=%fused_computation.140 | convolution fusion | flops 1614807040 | bytes 8916992 | tf_op jit(solution)/shard_map/dot_general | solution.py:43
  116.9 4.4 fusion.7
  121.2 8.3 %fusion.146 = f32[1024,512]{0,1:T(8,128)S(1)} fusion(f32[1024,512]{0,1:T(8,128)S(1)} %fusion.147, f32[1024,2048]{1,0:T(8,128)} %get-tuple-element.79, f32[1024]{0:T(1024)S(1)} %get-tuple-element.78, bf16[2048,512]{0,1:T(8,128)(2,1)S(1)} %copy-done.5), kind=kOutput, calls=%fused_computation.139 | convolution fusion | flops 1614807040 | bytes 8916992 | tf_op jit(solution)/shard_map/dot_general | solution.py:43
  131.5 5.5 %fusion.145 = f32[1024,512]{0,1:T(8,128)S(1)} fusion(f32[1024,512]{0,1:T(8,128)S(1)} %fusion.146, f32[1024,2048]{1,0:T(8,128)S(1)} %get-tuple-element.81, f32[1024]{0:T(1024)S(1)} %get-tuple-element.80, bf16[2048,512]{0,1:T(8,128)(2,1)S(1)} %copy-done.5), kind=kOutput, calls=%fused_computation.138 | convolution fusion | flops 1614807040 | bytes 8916992 | tf_op jit(solution)/shard_map/dot_general | solution.py:43
  139.3 5.5 %fusion.144 = f32[1024,512]{0,1:T(8,128)S(1)} fusion(f32[1024,512]{0,1:T(8,128)S(1)} %fusion.145, f32[1024,2048]{1,0:T(8,128)S(1)} %get-tuple-element.83, f32[1024]{0:T(1024)S(1)} %get-tuple-element.82, bf16[2048,512]{0,1:T(8,128)(2,1)S(1)} %copy-done.5), kind=kOutput, calls=%fused_computation.137 | convolution fusion | flops 1614807040 | bytes 8916992 | tf_op jit(solution)/shard_map/dot_general | solution.py:43
  146.8 5.5 %fusion.143 = f32[1024,512]{0,1:T(8,128)S(1)} fusion(f32[1024,512]{0,1:T(8,128)S(1)} %fusion.144, f32[1024,2048]{1,0:T(8,128)S(1)} %get-tuple-element.85, f32[1024]{0:T(1024)S(1)} %get-tuple-element.84, bf16[2048,512]{0,1:T(8,128)(2,1)S(1)} %copy-done.5), kind=kOutput, calls=%fused_computation.136 | convolution fusion | flops 1614807040 | bytes 8916992 | tf_op jit(solution)/shard_map/dot_general | solution.py:43
  154.4 5.5 %fusion.142 = f32[1024,512]{0,1:T(8,128)S(1)} fusion(f32[1024,512]{0,1:T(8,128)S(1)} %fusion.143, f32[1024,2048]{1,0:T(8,128)S(1)} %get-tuple-element.87, f32[1024]{0:T(1024)S(1)} %get-tuple-element.86, bf16[2048,512]{0,1:T(8,128)(2,1)S(1)} %copy-done.5), kind=kOutput, calls=%fused_computation.135 | convolution fusion | flops 1614807040 | bytes 8916992 | tf_op jit(solution)/shard_map/dot_general | solution.py:43
  160.0 2.4 slice_bitcast_fusion.19
  162.4 2.6 slice_bitcast_fusion
  168.8 9.7 %all-to-all-start.1 = ((f32[32,1,256]{2,1,0:T(1,128)}), f32[32,1,256]{2,1,0:T(1,128)}, u32[]{:S(2)}, u32[]{:S(2)}) async-start(f32[32,1,256]{2,1,0:T(1,128)} %reshape.90), calls=%async_computation.1 | async-start | bytes 65536 | tf_op jit(solution)/shard_map/all_to_all | solution.py:129
  237.1 5.9 %all-to-all-start.2 = ((f32[32,1,256]{2,1,0:T(1,128)}), f32[32,1,256]{2,1,0:T(1,128)S(1)}, u32[]{:S(2)}, u32[]{:S(2)}) async-start(f32[32,1,256]{2,1,0:T(1,128)} %reshape.92), calls=%async_computation.2 | async-start | bytes 65536 | tf_op jit(solution)/shard_map/all_to_all | solution.py:128
  243.7 6.6 %all-to-all-done.2 = f32[32,1,256]{2,1,0:T(1,128)S(1)} async-done(((f32[32,1,256]{2,1,0:T(1,128)}), f32[32,1,256]{2,1,0:T(1,128)S(1)}, u32[]{:S(2)}, u32[]{:S(2)}) %all-to-all-start.2) | async-done | bytes 32800 | tf_op jit(solution)/shard_map/all_to_all | solution.py:128
  250.3 3.5 all-to-all-start
  258.8 2.6 mul.442
  261.4 3.9 mul.443
  265.3 37.2 %all-to-all-done = f32[32,1,32,512]{3,2,1,0:T(8,128)} async-done(((f32[32,1,32,512]{3,2,1,0:T(8,128)}), f32[32,1,32,512]{3,2,1,0:T(8,128)}, u32[]{:S(2)}, u32[]{:S(2)}) %all-to-all-start) | async-done | bytes 2097184 | tf_op jit(solution)/shard_map/all_to_all | solution.py:120
  306.3 3.0 convolution_convert_fusion.2
  309.3 50.1 %all-gather.2.cloned.1.call-done = bf16[1024,512]{1,0:T(8,128)(2,1)} async-done(((bf16[32,512]{1,0:T(8,128)(2,1)}), bf16[1024,512]{1,0:T(8,128)(2,1)}) %all-gather.2.cloned.1.call-update) | async-done | bytes 1048592 | tf_op jit(solution)/shard_map/all_gather | solution.py:144
  365.3 4.5 multiply_reduce_fusion.3
  369.9 4.5 multiply_reduce_fusion.4
  374.4 4.5 multiply_reduce_fusion.5
  378.9 4.5 multiply_reduce_fusion.6
  383.4 4.7 %multiply_reduce_fusion.7 = (f32[2048]{0:T(1024)S(1)}, f32[2048,1024]{0,1:T(8,128)}) fusion(bf16[1024,512]{0,1:T(8,128)(2,1)S(1)} %convolution_convert_fusion.4, bf16[2048,512]{0,1:T(8,128)(2,1)S(1)} %convolution_convert_fusion.2), kind=kOutput, calls=%fused_computation.26 | convolution fusion | flops 272627712 | bytes 8790016 | tf_op jit(solution)/shard_map/dot_general | solution.py:33
  392.3 4.8 %fusion.25 = f32[2048]{0:T(1024)S(1)} fusion(f32[2048,1024]{0,1:T(8,128)} %get-tuple-element.97, f32[2048]{0:T(1024)S(1)} %get-tuple-element.96), kind=kLoop, calls=%fused_computation.59 | loop fusion | flops 6289408 | bytes 8404992 | tf_op jit(solution)/shard_map/reduce_sum | solution.py:157
  397.1 4.8 %fusion.23 = f32[2048]{0:T(1024)S(1)} fusion(f32[2048,1024]{0,1:T(8,128)} %get-tuple-element.95, f32[2048]{0:T(1024)S(1)} %get-tuple-element.94), kind=kLoop, calls=%fused_computation.57 | loop fusion | flops 6289408 | bytes 8404992 | tf_op jit(solution)/shard_map/reduce_sum | solution.py:157
  401.9 4.8 %fusion.21 = f32[2048]{0:T(1024)S(1)} fusion(f32[2048,1024]{0,1:T(8,128)} %get-tuple-element.93, f32[2048]{0:T(1024)S(1)} %get-tuple-element.92), kind=kLoop, calls=%fused_computation.55 | loop fusion | flops 6289408 | bytes 8404992 | tf_op jit(solution)/shard_map/reduce_sum | solution.py:157
  406.7 4.8 %fusion.19 = f32[2048]{0:T(1024)S(1)} fusion(f32[2048,1024]{0,1:T(8,128)} %get-tuple-element.91, f32[2048]{0:T(1024)S(1)} %get-tuple-element.90), kind=kLoop, calls=%fused_computation.53 | loop fusion | flops 6289408 | bytes 8404992 | tf_op jit(solution)/shard_map/reduce_sum | solution.py:157
  411.5 5.1 %fusion.17 = f32[2048]{0:T(1024)S(1)} fusion(f32[2048,1024]{0,1:T(8,128)} %get-tuple-element.89, f32[2048]{0:T(1024)S(1)} %get-tuple-element.88), kind=kLoop, calls=%fused_computation.51 | loop fusion | flops 6289408 | bytes 8404992 | tf_op jit(solution)/shard_map/reduce_sum | solution.py:157
  417.4 4.9 %fusion.76 = bf16[2048,512]{0,1:T(8,128)(2,1)S(1)} fusion(f32[2048,1024]{0,1:T(8,128)} %get-tuple-element.89, f32[2048]{0:T(1024)S(1)} %get-tuple-element.88, f32[2048]{0:T(1024)S(1)} %fusion.17, bf16[1024,512]{0,1:T(8,128)(2,1)S(1)} %convolution_convert_fusion.3), kind=kOutput, calls=%fused_computation.107 | convolution fusion | flops 274989056 | bytes 8798208 | tf_op jit(solution)/shard_map/dot_general | solution.py:158
  422.3 4.9 %fusion.85 = bf16[2048,512]{0,1:T(8,128)(2,1)S(1)} fusion(bf16[2048,512]{0,1:T(8,128)(2,1)S(1)} %fusion.76, f32[2048,1024]{0,1:T(8,128)} %get-tuple-element.91, f32[2048]{0:T(1024)S(1)} %get-tuple-element.90, f32[2048]{0:T(1024)S(1)} %fusion.19, bf16[1024,512]{0,1:T(8,128)(2,1)S(1)} %convolution_convert_fusion.3), kind=kOutput, calls=%fused_computation.110 | convolution fusion | flops 274989056 | bytes 8798208 | tf_op jit(solution)/shard_map/dot_general | solution.py:158
  427.2 5.1 %fusion.94 = bf16[2048,512]{0,1:T(8,128)(2,1)S(1)} fusion(bf16[2048,512]{0,1:T(8,128)(2,1)S(1)} %fusion.85, f32[2048,1024]{0,1:T(8,128)} %get-tuple-element.93, f32[2048]{0:T(1024)S(1)} %get-tuple-element.92, f32[2048]{0:T(1024)S(1)} %fusion.21, bf16[1024,512]{0,1:T(8,128)(2,1)S(1)} %convolution_convert_fusion.3), kind=kOutput, calls=%fused_computation.113 | convolution fusion | flops 274989056 | bytes 8798208 | tf_op jit(solution)/shard_map/dot_general | solution.py:158
  432.3 5.1 %fusion.103 = bf16[2048,512]{0,1:T(8,128)(2,1)S(1)} fusion(bf16[2048,512]{0,1:T(8,128)(2,1)S(1)} %fusion.94, f32[2048,1024]{0,1:T(8,128)} %get-tuple-element.95, f32[2048]{0:T(1024)S(1)} %get-tuple-element.94, f32[2048]{0:T(1024)S(1)} %fusion.23, bf16[1024,512]{0,1:T(8,128)(2,1)S(1)} %convolution_convert_fusion.3), kind=kOutput, calls=%fused_computation.116 | convolution fusion | flops 274989056 | bytes 8798208 | tf_op jit(solution)/shard_map/dot_general | solution.py:158
  443.8 3.3 bitcast_add_fusion
  (163 shorter events, 112.5 us)
Async XLA Ops:
  6.5 45.5 %copy-start = (bf16[512,512]{1,0:T(8,128)(2,1)S(1)}, bf16[512,512]{1,0:T(8,128)(2,1)}, u32[]{:S(2)}) copy-start(bf16[512,512]{1,0:T(8,128)(2,1)} %param.17) | copy-start | bytes 1572868
  6.5 9.2 %copy-start.10 = (f32[27,512]{1,0:T(8,128)S(1)}, f32[27,512]{1,0:T(8,128)}, u32[]{:S(2)}) copy-start(f32[27,512]{1,0:T(8,128)} %param.14) | copy-start | bytes 165892
  6.5 9.2 %copy-start.11 = (bf16[1024,512]{1,0:T(8,128)(2,1)S(1)}, bf16[1024,512]{1,0:T(8,128)(2,1)}, u32[]{:S(2)}) copy-start(bf16[1024,512]{1,0:T(8,128)(2,1)} %param.15) | copy-start | bytes 3145732
  6.5 9.2 %copy-start.13 = (bf16[512,512]{1,0:T(8,128)(2,1)S(1)}, bf16[512,512]{1,0:T(8,128)(2,1)}, u32[]{:S(2)}) copy-start(bf16[512,512]{1,0:T(8,128)(2,1)} %param.16) | copy-start | bytes 1572868
  9.5 26.2 %copy-start.2 = (bf16[8,16,16,512]{3,2,1,0:T(8,128)(2,1)}, bf16[8,16,16,512]{3,2,1,0:T(8,128)(2,1)S(1)}, u32[]{:S(2)}) copy-start(bf16[8,16,16,512]{3,2,1,0:T(8,128)(2,1)S(1)} %broadcast_multiply_fusion) | copy-start | bytes 6291460
  9.5 16.0 %collective-permute-start = (bf16[1,16,16,512]{3,2,1,0:T(8,128)(2,1)S(1)}, bf16[1,16,16,512]{3,2,1,0:T(8,128)(2,1)S(1)}, u32[]{:S(2)}, u32[]{:S(2)}) collective-permute-start(bf16[1,16,16,512]{3,2,1,0:T(8,128)(2,1)S(1)} %get-tuple-element.43), channel_id=1, source_target_pairs={{0,4},{4,8},{8,12},{12,16},{16,20},{20,24},{24,28},{1,5},{5,9},{9,... | collective-permute-start | bytes 786440 | tf_op jit(solution)/shard_map/ppermute | solution.py:18
  14.4 11.2 %collective-permute-start.1 = (bf16[1,16,16,512]{3,2,1,0:T(8,128)(2,1)S(1)}, bf16[1,16,16,512]{3,2,1,0:T(8,128)(2,1)S(1)}, u32[]{:S(2)}, u32[]{:S(2)}) collective-permute-start(bf16[1,16,16,512]{3,2,1,0:T(8,128)(2,1)S(1)} %get-tuple-element.44), channel_id=1, source_target_pairs={{4,0},{8,4},{12,8},{16,12},{20,16},{24,20},{28,24},{5,1},{9,5},{13... | collective-permute-start | bytes 786440 | tf_op jit(solution)/shard_map/ppermute | solution.py:20
  25.6 2.6 collective-permute-start.2
  26.9 5.0 %collective-permute-start.3 = (bf16[10,1,16,512]{3,2,1,0:T(8,128)(2,1)S(1)}, bf16[10,1,16,512]{3,2,1,0:T(8,128)(2,1)S(1)}, u32[]{:S(2)}, u32[]{:S(2)}) collective-permute-start(bf16[10,1,16,512]{3,2,1,0:T(8,128)(2,1)S(1)} %get-tuple-element.10), channel_id=1, source_target_pairs={{1,0},{2,1},{3,2},{5,4},{6,5},{7,6},{9,8},{10,9},{11,10},{13,12},{... | collective-permute-start | bytes 491528 | tf_op jit(solution)/shard_map/ppermute | solution.py:20
  52.1 24.7 %copy-start.4 = (bf16[8,16,16,512]{3,2,1,0:T(8,128)(2,1)}, bf16[8,16,16,512]{3,2,1,0:T(8,128)(2,1)S(1)}, u32[]{:S(2)}) copy-start(bf16[8,16,16,512]{3,2,1,0:T(8,128)(2,1)S(1)} %add_convert_fusion) | copy-start | bytes 6291460
  72.3 4.5 copy-start.14
  79.6 4.5 copy-start.5
  168.8 68.3 %all-to-all-start.1 = ((f32[32,1,256]{2,1,0:T(1,128)}), f32[32,1,256]{2,1,0:T(1,128)}, u32[]{:S(2)}, u32[]{:S(2)}) async-start(f32[32,1,256]{2,1,0:T(1,128)} %reshape.90), calls=%async_computation.1 | async-start | bytes 65536 | tf_op jit(solution)/shard_map/all_to_all | solution.py:129
  180.9 29.8 %copy-start.7 = (f32[1,1,32,512]{2,3,1,0:T(8,128)S(1)}, f32[1,1,32,512]{2,3,1,0:T(8,128)}, u32[]{:S(2)}) copy-start(f32[1,1,32,512]{2,3,1,0:T(8,128)} %get-tuple-element.20) | copy-start | bytes 196612
  180.9 29.9 %copy-start.6 = (f32[1,1,32,512]{2,3,1,0:T(8,128)S(1)}, f32[1,1,32,512]{2,3,1,0:T(8,128)}, u32[]{:S(2)}) copy-start(f32[1,1,32,512]{2,3,1,0:T(8,128)} %get-tuple-element.21) | copy-start | bytes 196612
  237.1 13.2 %all-to-all-start.2 = ((f32[32,1,256]{2,1,0:T(1,128)}), f32[32,1,256]{2,1,0:T(1,128)S(1)}, u32[]{:S(2)}, u32[]{:S(2)}) async-start(f32[32,1,256]{2,1,0:T(1,128)} %reshape.92), calls=%async_computation.2 | async-start | bytes 65536 | tf_op jit(solution)/shard_map/all_to_all | solution.py:128
  250.3 52.2 %all-to-all-start = ((f32[32,1,32,512]{3,2,1,0:T(8,128)}), f32[32,1,32,512]{3,2,1,0:T(8,128)}, u32[]{:S(2)}, u32[]{:S(2)}) async-start(f32[32,1,32,512]{3,2,1,0:T(8,128)} %constant_dynamic-update-slice_fusion), calls=%async_computation | async-start | bytes 4194304 | tf_op jit(solution)/shard_map/all_to_all | solution.py:120
  253.8 105.6 %all-gather.2.cloned.1.call-start = ((), (), s32[]{:S(2)}) async-start(), calls=%async_computation.3 | async-start | bytes 1081344 | tf_op jit(solution)/shard_map/all_gather | solution.py:144
  261.4 43.2 %copy-start.9 = (bf16[512,512]{1,0:T(8,128)(2,1)S(1)}, bf16[512,512]{1,0:T(8,128)(2,1)}, u32[]{:S(2)}) copy-start(bf16[512,512]{1,0:T(8,128)(2,1)} %param.19) | copy-start | bytes 1572868
  306.2 53.2 %copy-start.15 = (bf16[512,512]{1,0:T(8,128)(2,1)S(1)}, bf16[512,512]{1,0:T(8,128)(2,1)}, u32[]{:S(2)}) copy-start(bf16[512,512]{1,0:T(8,128)(2,1)} %param.21) | copy-start | bytes 1572868
  411.5 5.1 %copy-start.12 = (bf16[1024,512]{1,0:T(8,128)(2,1)S(1)}, bf16[1024,512]{1,0:T(8,128)(2,1)}, u32[]{:S(2)}) copy-start(bf16[1024,512]{1,0:T(8,128)(2,1)} %all-gather.2.cloned.1.call-done) | copy-start | bytes 3145732
  411.5 5.1 %copy-start.16 = (bf16[512,512]{1,0:T(8,128)(2,1)S(1)}, bf16[512,512]{1,0:T(8,128)(2,1)}, u32[]{:S(2)}) copy-start(bf16[512,512]{1,0:T(8,128)(2,1)} %param.22) | copy-start | bytes 1572868
  427.2 10.2 %slice-start = ((s8[8388608]{0:T(1024)(128)(4,1)}), s8[4194304]{0:T(1024)(128)(4,1)S(1)}, s32[]{:S(2)}) async-start(s8[8388608]{0:T(1024)(128)(4,1)} %bitcast.142), calls=%async_computation.4 | async-start | bytes 8388608
  432.3 5.1 %slice-start.1 = ((s8[8388608]{0:T(1024)(128)(4,1)}), s8[4194304]{0:T(1024)(128)(4,1)S(1)}, s32[]{:S(2)}) async-start(s8[8388608]{0:T(1024)(128)(4,1)} %bitcast.142), calls=%async_computation.5 | async-start | bytes 8388608
  442.1 1.6 copy-start.3
  442.1 1.7 copy-start.8
  442.1 5.0 %copy-start.1 = (bf16[512,512]{1,0:T(8,128)(2,1)S(1)}, bf16[512,512]{1,0:T(8,128)(2,1)}, u32[]{:S(2)}) copy-start(bf16[512,512]{1,0:T(8,128)(2,1)} %param.17) | copy-start | bytes 1572868
Sparse Core Ops, SparseCore 0:
  306.4 53.0 all-gather.1
